TPU v7x, 32 devices: a whole 2x2x4 slice. The times are simulated.
32 devices in a mesh: row: 8 (over z, core), col: 4 (over y, x).
Axes of the slice: x: 2, y: 2, z: 4, core: 2. Of those that a mesh axis runs over, the one named last changes fastest.
Arguments:
- matrix: float32 [8192, 4096], P('row', 'col'), may hold values from -6 to 166
Outputs:
- updated: float32 [8192, 4096], P('row', 'col')
All inputs are finite; a program needn't handle non-finite values.
Results may differ from a plain program's by a relative error of at most 0.0003.
Values sent between devices are 32-bit elements; how exact they have to be, the bound alone decides.
No kernel may reach another device: no remote copies, remote signals or barrier semaphores. Data moves between devices by JAX's collectives and lax.ppermute only.
A program may use at most 64 MiB of HBM per device.

v0:
```python
import jax
import jax.numpy as jnp
from jax import lax
from jax.sharding import PartitionSpec as P

NB = 128


def from_root(value, axis, source):
    kept = jnp.where(lax.axis_index(axis) == source, value, 0).astype(value.dtype)
    return lax.psum(kept, axis)


def factor(corner):
    symmetric = jnp.tril(corner) + jnp.tril(corner, -1).T
    lower_factor = jnp.linalg.cholesky(symmetric)
    identity = jnp.eye(corner.shape[0], dtype=jnp.float32)
    inverse = jax.scipy.linalg.solve_triangular(lower_factor, identity, lower=True)
    return (lower_factor, inverse)


def body(matrix):
    rows_here = lax.axis_size("row")
    cols_here = lax.axis_size("col")
    row_index = lax.axis_index("row")
    col_index = lax.axis_index("col")
    row_blocks = matrix.shape[0] // NB
    col_blocks = matrix.shape[1] // NB
    corner = matrix[:NB, :NB]
    local_factor, local_inverse = factor(corner)
    stacked = from_root(jnp.stack([local_factor, local_inverse]), "row", 0)
    lower_factor = stacked[0]
    inverse = stacked[1]
    panel = lax.dot_general(
        matrix[:, :NB],
        inverse,
        (((1,), (1,)), ((), ())),
        precision=lax.Precision.HIGHEST,
        preferred_element_type=jnp.float32,
    )
    panel = panel.at[:NB].set(jnp.where(row_index == 0, lower_factor, panel[:NB]))
    panel = from_root(panel, "col", 0)
    whole = lax.all_gather(panel, "row", axis=0, tiled=True)
    all_blocks = whole.reshape(rows_here * row_blocks, NB, NB)
    wanted = jnp.arange(col_blocks, dtype=jnp.int32) * cols_here + col_index
    source_rows = wanted % rows_here * row_blocks + wanted // rows_here
    mirror = jnp.take(all_blocks, source_rows, axis=0).reshape(col_blocks * NB, NB)
    product = lax.dot_general(
        panel,
        mirror,
        (((1,), (1,)), ((), ())),
        precision=lax.Precision.HIGHEST,
        preferred_element_type=jnp.float32,
    )
    fresh = matrix - product
    global_rows = jnp.arange(row_blocks, dtype=jnp.int32) * rows_here + row_index
    global_cols = jnp.arange(col_blocks, dtype=jnp.int32) * cols_here + col_index
    keep_mask = (global_rows[:, None] >= global_cols[None, :]) & (global_cols[None, :] >= 1)
    shaped_old = matrix.reshape(row_blocks, NB, col_blocks, NB)
    shaped_new = fresh.reshape(row_blocks, NB, col_blocks, NB)
    result = jnp.where(keep_mask[:, None, :, None], shaped_new, shaped_old).reshape(matrix.shape)
    result = result.at[:, :NB].set(jnp.where(col_index == 0, panel, result[:, :NB]))
    return result


def solution(mesh):
    return jax.shard_map(
        body, mesh=mesh, in_specs=(P("row", "col"),), out_specs=P("row", "col"), check_vma=False
    )
```

profile of v0, /device:TPU:0, one launch (start us, length us, event | category | flops | bytes accessed | tf_op | source)
XLA Modules:
  0.0 205.8 jit_solution(1696970586358199093)
XLA Ops:
  6.5 0.8 slice.64
  7.4 0.1 copy.8
  7.5 0.9 bitcast_add_fusion.1
  8.3 0.1 copy.5
  8.5 11.7 %cholesky.19 = f32[128,128]{1,0:T(8,128)S(1)} custom-call(f32[128,128]{1,0:T(8,128)S(1)} %fusion.4), custom_call_target="Cholesky" | custom-call | tf_op jit(solution)/shard_map/jit(cholesky)/cholesky | solution.py:16
  20.2 0.6 compare_reduce_fusion.1
  20.9 0.7 fusion.5
  21.5 9.8 %custom-call.7 = f32[1,128,128]{1,2,0:T(8,128)S(1)} custom-call(f32[1,128,128]{2,1,0:T(8,128)S(1)} %get-tuple-element.30), custom_call_target="InvertDiagBlocksLowerTriangular" | custom-call | tf_op jit(solution)/shard_map/jit(_solve_triangular)/triangular_solve | solution.py:18
  31.3 0.2 convolution_bitcast_fusion.1
  31.6 0.7 maximum_select_fusion
  32.3 57.0 %all-reduce.3.cloned.1.call-done = f32[2,128,128]{2,1,0:T(8,128)} async-done(((f32[2,128,128]{2,1,0:T(8,128)}), f32[2,128,128]{2,1,0:T(8,128)}) %all-reduce.3.cloned.1.call-update) | async-done | bytes 131088 | tf_op jit(solution)/shard_map/psum | solution.py:11
  89.3 1.7 convolution_bitcast_fusion
  91.0 0.9 fusion.2
  91.8 0.8 broadcast_select_fusion
  92.8 44.4 %all-reduce.5.cloned.1.call-done = f32[1024,128]{1,0:T(8,128)} async-done(((f32[1024,128]{1,0:T(8,128)}), f32[1024,128]{1,0:T(8,128)}) %all-reduce.5.cloned.1.call-update) | async-done | bytes 524304 | tf_op jit(solution)/shard_map/psum | solution.py:11
  137.2 0.6 compare_reduce_fusion
  137.9 0.1 broadcast_bitcast_fusion
  138.0 0.1 compare_and_fusion
  138.1 48.0 %all-gather.2.cloned.1.call-done = f32[8192,128]{1,0:T(8,128)} async-done(((f32[1024,128]{1,0:T(8,128)}), f32[8192,128]{1,0:T(8,128)}) %all-gather.2.cloned.1.call-update) | async-done | bytes 4194320 | tf_op jit(solution)/shard_map/all_gather | solution.py:43
  186.1 2.8 %gather_fusion = f32[8,128,128]{2,1,0:T(8,128)S(1)} fusion(f32[64,128,128]{2,1,0:T(8,128)} %bitcast.38, s32[1024]{0:T(1024)S(1)} %pad_clamp_fusion), kind=kCustom, calls=%fused_computation | custom fusion | bytes 1048608 | tf_op jit(solution)/shard_map/jit(_take)/gather | solution.py:47
  188.8 0.2 bitcast_select_fusion
  189.0 0.3 broadcast_in_dim.44
  189.4 7.4 %subtract_select_fusion = f32[1024,1024]{1,0:T(8,128)} fusion(f32[1024,1024]{1,0:T(8,128)} %param.5, pred[128,8,8,128]{3,2,1,0:T(8,128)(4,1)S(1)} %bitcast.37, f32[1024,128]{1,0:T(8,128)} %all-reduce.5.cloned.1.call-done, f32[1024,128]{1,0:T(8,128)S(1)} %bitcast_select_fusion), kind=kOutput, calls=%fused_computation.1 | convolution fusion | flops 1612709888 | bytes 10485760 | tf_op jit(solution)/shard_map/dot_general | solution.py:48
  196.8 2.5 %fusion = f32[1024,1024]{1,0:T(8,128)} fusion(f32[1024,1024]{1,0:T(8,128)} %subtract_select_fusion, f32[1024,128]{1,0:T(8,128)S(1)} %copy-done, pred[]{:T(512)} %compare_reduce_fusion, pred[]{:T(512)S(6)} %eq.6), kind=kLoop, calls=%fused_computation.5 | loop fusion | flops 262144 | bytes 1573377 | tf_op jit(solution)/shard_map/scatter | solution.py:62
  (17 shorter events, 0.2 us)
Async XLA Ops:
  6.5 82.8 %all-reduce.3.cloned.1.call-start = ((), (), s32[]{:S(2)}) async-start(), calls=%async_computation | async-start | bytes 262144 | tf_op jit(solution)/shard_map/psum | solution.py:11
  32.3 104.9 %all-reduce.5.cloned.1.call-start = ((), (), s32[]{:S(2)}) async-start(), calls=%async_computation.1 | async-start | bytes 1048576 | tf_op jit(solution)/shard_map/psum | solution.py:11
  92.7 93.4 %all-gather.2.cloned.1.call-start = ((), (), s32[]{:S(2)}) async-start(), calls=%async_computation.2 | async-start | bytes 4718592 | tf_op jit(solution)/shard_map/all_gather | solution.py:43
  189.4 7.4 %copy-start = (f32[1024,128]{1,0:T(8,128)S(1)}, f32[1024,128]{1,0:T(8,128)}, u32[]{:S(2)}) copy-start(f32[1024,128]{1,0:T(8,128)} %all-reduce.5.cloned.1.call-done) | copy-start | bytes 1572868
Sparse Core Ops, SparseCore 0:
  32.4 56.8 all-reduce.2
  92.8 44.3 all-reduce.4
  138.9 47.1 all-gather.1
where the time goes:
time: 206 us
  waiting for transfers between devices  149 us (72%)
  other arithmetic  29.5 us (14%)
  between operations  13.2 us (6%)
  matrix products  9.34 us (5%)
  local copies, waits for them, and re-layouts  4.2 us (2%)
    psum x2, waiting for transfers between devices, from_root(): return lax.psum(kept, axis)  101 us
    all_gather x1, waiting for transfers between devices, body(): whole = lax.all_gather(panel, 'row', axis=0, tiled=True)  48 us
    another operation x3, other arithmetic, factor(): lower_factor = jnp.linalg.cholesky(symmetric)  12.4 us
    another operation x1, other arithmetic, factor(): jax.scipy.linalg.solve_triangular(lower_factor, identity, lower=True)  9.81 us
    dot_general x1, matrix products, body(): lax.dot_general(panel, mirror, (((1,), (1,)), ((), ())), precision=lax.Pr...  7.43 us
  transfers between devices with their start and end apart: 3, of which 3 were waited for; matrix products, arithmetic and copies ran while one was open for 0% of the time, Pallas kernels for 0%

commit v1 on v0

--- a/solution.py
+++ b/solution.py
@@ -4,6 +4,27 @@
 from jax.sharding import PartitionSpec as P
 
 NB = 128
+
+
+def ring_gather(x, axis, dim):
+    peers, index, span = (lax.axis_size(axis), lax.axis_index(axis), x.shape[dim])
+    ahead = [(i, (i + 1) % peers) for i in range(peers)]
+    backward = [(i, (i - 1) % peers) for i in range(peers)]
+    whole = jnp.zeros((*x.shape[:dim], peers * span, *x.shape[dim + 1 :]), x.dtype)
+    whole = lax.dynamic_update_slice_in_dim(whole, x, index * span, axis=dim)
+    from_left = from_right = x
+    halfway = peers // 2
+    for turn in range(1, halfway + 1):
+        from_left = lax.ppermute(from_left, axis, ahead)
+        whole = lax.dynamic_update_slice_in_dim(
+            whole, from_left, (index - turn) % peers * span, axis=dim
+        )
+        if turn < peers - halfway:
+            from_right = lax.ppermute(from_right, axis, backward)
+            whole = lax.dynamic_update_slice_in_dim(
+                whole, from_right, (index + turn) % peers * span, axis=dim
+            )
+    return whole
 
 
 def from_root(value, axis, source):
@@ -40,7 +61,7 @@
     )
     panel = panel.at[:NB].set(jnp.where(row_index == 0, lower_factor, panel[:NB]))
     panel = from_root(panel, "col", 0)
-    whole = lax.all_gather(panel, "row", axis=0, tiled=True)
+    whole = ring_gather(panel, "row", 0)
     all_blocks = whole.reshape(rows_here * row_blocks, NB, NB)
     wanted = jnp.arange(col_blocks, dtype=jnp.int32) * cols_here + col_index
     source_rows = wanted % rows_here * row_blocks + wanted // rows_here

time: 206 us -> 214 us (1.039)
  waiting for transfers between devices: 149 us -> 138 us
  starting transfers between devices: 0.09 us -> 10.7 us
  local copies, waits for them, and re-layouts: 4.2 us -> 13.1 us
    all_gather x1 -> x0, waiting for transfers between devices: 48 us -> none  [body(): whole = lax.all_gather(panel, 'row', axis=0, tiled=True)]
    ppermute x0 -> x7, waiting for transfers between devices: none -> 36.7 us  [the longest x4 36.7 us: ring_gather(): from_left = lax.ppermute(from_left, axis, ahead)]
    ppermute x0 -> x7, starting transfers between devices: none -> 10.7 us  [the longest x3 10.7 us: ring_gather(): from_right = lax.ppermute(from_right, axis, backward)]
    dynamic_update_slice x0 -> x8, local copies, waits for them, and re-layouts: none -> 6.61 us  [the longest x4 3.31 us: ring_gather(): lax.dynamic_update_slice_in_dim(whole, from_left, (index - turn) % peers...]
    broadcast_in_dim x0 -> x1, local copies, waits for them, and re-layouts: none -> 2.28 us  [ring_gather(): jnp.zeros((*x.shape[:dim], peers * span, *x.shape[dim + 1:]), x.dtype)]
  transfers between devices with their start and end apart: 3 -> 9, of which waited for: 3 -> 6; matrix products, arithmetic and copies ran while one was open for 0% -> 4% of each run, Pallas kernels for 0% -> 0%
where the time goes in v1:
time: 214 us
  waiting for transfers between devices  138 us (64%)
  other arithmetic  29.5 us (14%)
  between operations  13.5 us (6%)
  local copies, waits for them, and re-layouts  13.1 us (6%)
  starting transfers between devices  10.7 us (5%)
  matrix products  8.89 us (4%)
    psum x2, waiting for transfers between devices, from_root(): return lax.psum(kept, axis)  101 us
    ppermute x4, waiting for transfers between devices, ring_gather(): from_left = lax.ppermute(from_left, axis, ahead)  36.7 us
    another operation x3, other arithmetic, factor(): lower_factor = jnp.linalg.cholesky(symmetric)  12.4 us
    ppermute x3, starting transfers between devices, ring_gather(): from_right = lax.ppermute(from_right, axis, backward)  10.7 us
    another operation x1, other arithmetic, factor(): jax.scipy.linalg.solve_triangular(lower_factor, identity, lower=True)  9.81 us
    dot_general x1, matrix products, body(): lax.dot_general(panel, mirror, (((1,), (1,)), ((), ())), precision=lax.Pr...  6.97 us
  transfers between devices with their start and end apart: 9, of which 6 were waited for; matrix products, arithmetic and copies ran while one was open for 4% of the time, Pallas kernels for 0%

profile of v1, /device:TPU:0, one launch (start us, length us, event | category | flops | bytes accessed | tf_op | source)
XLA Modules:
  0.0 213.9 jit_solution(17150203559193433912)
XLA Ops:
  6.5 0.8 slice.64
  7.5 0.9 bitcast_add_fusion.1
  8.5 11.7 %cholesky.19 = f32[128,128]{1,0:T(8,128)S(1)} custom-call(f32[128,128]{1,0:T(8,128)S(1)} %fusion.4), custom_call_target="Cholesky" | custom-call | tf_op jit(solution)/shard_map/jit(cholesky)/cholesky | solution.py:37
  21.5 9.8 %custom-call.7 = f32[1,128,128]{1,2,0:T(8,128)S(1)} custom-call(f32[1,128,128]{2,1,0:T(8,128)S(1)} %get-tuple-element.30), custom_call_target="InvertDiagBlocksLowerTriangular" | custom-call | tf_op jit(solution)/shard_map/jit(_solve_triangular)/triangular_solve | solution.py:39
  32.3 57.0 %all-reduce.3.cloned.1.call-done = f32[2,128,128]{2,1,0:T(8,128)} async-done(((f32[2,128,128]{2,1,0:T(8,128)}), f32[2,128,128]{2,1,0:T(8,128)}) %all-reduce.3.cloned.1.call-update) | async-done | bytes 131088 | tf_op jit(solution)/shard_map/psum | solution.py:32
  89.3 1.7 convolution_bitcast_fusion
  91.0 0.9 fusion.2
  91.8 0.8 broadcast_select_fusion
  92.7 44.5 %all-reduce.5.cloned.1.call-done = f32[1024,128]{1,0:T(8,128)} async-done(((f32[1024,128]{1,0:T(8,128)}), f32[1024,128]{1,0:T(8,128)}) %all-reduce.5.cloned.1.call-update) | async-done | bytes 524304 | tf_op jit(solution)/shard_map/psum | solution.py:32
  137.2 3.6 %collective-permute-start.1 = (f32[1024,128]{1,0:T(8,128)}, f32[1024,128]{1,0:T(8,128)S(1)}, u32[]{:S(2)}, u32[]{:S(2)}) collective-permute-start(f32[1024,128]{1,0:T(8,128)} %all-reduce.5.cloned.1.call-done), channel_id=1, source_target_pairs={{0,28},{4,0},{8,4},{12,8},{16,12},{20,16},{24,20},{28,24},{1,29},{... | collective-permute-start | bytes 1572872 | tf_op jit(solution)/shard_map/ppermute | solution.py:23
  140.8 10.6 %collective-permute-done = f32[1024,128]{1,0:T(8,128)S(1)} collective-permute-done((f32[1024,128]{1,0:T(8,128)}, f32[1024,128]{1,0:T(8,128)S(1)}, u32[]{:S(2)}, u32[]{:S(2)}) %collective-permute-start) | collective-permute-done | bytes 524320 | tf_op jit(solution)/shard_map/ppermute | solution.py:18
  151.6 3.5 %collective-permute-start.3 = (f32[1024,128]{1,0:T(8,128)S(1)}, f32[1024,128]{1,0:T(8,128)S(1)}, u32[]{:S(2)}, u32[]{:S(2)}) collective-permute-start(f32[1024,128]{1,0:T(8,128)S(1)} %collective-permute-done.1), channel_id=1, source_target_pairs={{0,28},{4,0},{8,4},{12,8},{16,12},{20,16},{24,20},{28,24},{1,29},{... | collective-permute-start | bytes 1572872 | tf_op jit(solution)/shard_map/ppermute | solution.py:23
  155.1 12.2 %collective-permute-done.2 = f32[1024,128]{1,0:T(8,128)S(1)} collective-permute-done((f32[1024,128]{1,0:T(8,128)S(1)}, f32[1024,128]{1,0:T(8,128)S(1)}, u32[]{:S(2)}, u32[]{:S(2)}) %collective-permute-start.2) | collective-permute-done | bytes 524320 | tf_op jit(solution)/shard_map/ppermute | solution.py:18
  168.0 2.3 %broadcast_in_dim.55 = f32[8192,128]{1,0:T(8,128)} broadcast(f32[]{:T(128)} %constant.193.clone.1), dimensions={} | broadcast | bytes 4194308 | tf_op jit(solution)/shard_map/broadcast_in_dim | solution.py:13
  170.3 0.8 constant_dynamic-update-slice_fusion.7
  171.1 3.5 %collective-permute-start.5 = (f32[1024,128]{1,0:T(8,128)S(1)}, f32[1024,128]{1,0:T(8,128)S(1)}, u32[]{:S(2)}, u32[]{:S(2)}) collective-permute-start(f32[1024,128]{1,0:T(8,128)S(1)} %collective-permute-done.3), channel_id=1, source_target_pairs={{0,28},{4,0},{8,4},{12,8},{16,12},{20,16},{24,20},{28,24},{1,29},{... | collective-permute-start | bytes 1572872 | tf_op jit(solution)/shard_map/ppermute | solution.py:23
  175.5 7.6 %collective-permute-done.4 = f32[1024,128]{1,0:T(8,128)S(1)} collective-permute-done((f32[1024,128]{1,0:T(8,128)S(1)}, f32[1024,128]{1,0:T(8,128)S(1)}, u32[]{:S(2)}, u32[]{:S(2)}) %collective-permute-start.4) | collective-permute-done | bytes 524320 | tf_op jit(solution)/shard_map/ppermute | solution.py:18
  183.1 0.8 constant_dynamic-update-slice_fusion.5
  186.4 0.8 constant_dynamic-update-slice_fusion.1
  187.2 6.3 %collective-permute-done.6 = f32[1024,128]{1,0:T(8,128)S(1)} collective-permute-done((f32[1024,128]{1,0:T(8,128)S(1)}, f32[1024,128]{1,0:T(8,128)S(1)}, u32[]{:S(2)}, u32[]{:S(2)}) %collective-permute-start.6) | collective-permute-done | bytes 524320 | tf_op jit(solution)/shard_map/ppermute | solution.py:18
  193.5 0.8 constant_dynamic-update-slice_fusion
  194.3 2.8 %gather_fusion = f32[8,128,128]{2,1,0:T(8,128)S(1)} fusion(f32[64,128,128]{2,1,0:T(8,128)} %bitcast.10, s32[1024]{0:T(1024)S(1)} %pad_clamp_fusion), kind=kCustom, calls=%fused_computation | custom fusion | bytes 1048608 | tf_op jit(solution)/shard_map/jit(_take)/gather | solution.py:68
  197.7 7.0 %subtract_select_fusion = f32[1024,1024]{1,0:T(8,128)} fusion(f32[1024,1024]{1,0:T(8,128)} %param.5, pred[128,8,8,128]{3,2,1,0:T(8,128)(4,1)S(1)} %bitcast.37, f32[1024,128]{1,0:T(8,128)S(1)} %copy-done, f32[1024,128]{1,0:T(8,128)S(1)} %bitcast_select_fusion), kind=kOutput, calls=%fused_computation.1 | convolution fusion | flops 1612709888 | bytes 10485760 | tf_op jit(solution)/shard_map/dot_general | solution.py:69
  204.6 2.5 %fusion = f32[1024,1024]{1,0:T(8,128)} fusion(f32[1024,1024]{1,0:T(8,128)} %subtract_select_fusion, f32[1024,128]{1,0:T(8,128)S(1)} %copy-done, pred[]{:T(512)} %compare_reduce_fusion, pred[]{:T(512)S(6)} %eq.19), kind=kLoop, calls=%fused_computation.5 | loop fusion | flops 262144 | bytes 1573377 | tf_op jit(solution)/shard_map/scatter | solution.py:83
  (37 shorter events, 7.2 us)
Async XLA Ops:
  6.5 82.8 %all-reduce.3.cloned.1.call-start = ((), (), s32[]{:S(2)}) async-start(), calls=%async_computation | async-start | bytes 262144 | tf_op jit(solution)/shard_map/psum | solution.py:32
  32.3 104.9 %all-reduce.5.cloned.1.call-start = ((), (), s32[]{:S(2)}) async-start(), calls=%async_computation.1 | async-start | bytes 1048576 | tf_op jit(solution)/shard_map/psum | solution.py:32
  137.2 33.1 %copy-start = (f32[1024,128]{1,0:T(8,128)S(1)}, f32[1024,128]{1,0:T(8,128)}, u32[]{:S(2)}) copy-start(f32[1024,128]{1,0:T(8,128)} %all-reduce.5.cloned.1.call-done) | copy-start | bytes 1572868
  137.2 14.3 %collective-permute-start = (f32[1024,128]{1,0:T(8,128)}, f32[1024,128]{1,0:T(8,128)S(1)}, u32[]{:S(2)}, u32[]{:S(2)}) collective-permute-start(f32[1024,128]{1,0:T(8,128)} %all-reduce.5.cloned.1.call-done), channel_id=1, source_target_pairs={{0,4},{4,8},{8,12},{12,16},{16,20},{20,24},{24,28},{28,0},{1,5},{5... | collective-permute-start | bytes 1572872 | tf_op jit(solution)/shard_map/ppermute | solution.py:18
  137.2 14.3 %collective-permute-start.1 = (f32[1024,128]{1,0:T(8,128)}, f32[1024,128]{1,0:T(8,128)S(1)}, u32[]{:S(2)}, u32[]{:S(2)}) collective-permute-start(f32[1024,128]{1,0:T(8,128)} %all-reduce.5.cloned.1.call-done), channel_id=1, source_target_pairs={{0,28},{4,0},{8,4},{12,8},{16,12},{20,16},{24,20},{28,24},{1,29},{... | collective-permute-start | bytes 1572872 | tf_op jit(solution)/shard_map/ppermute | solution.py:23
  151.5 15.9 %collective-permute-start.2 = (f32[1024,128]{1,0:T(8,128)S(1)}, f32[1024,128]{1,0:T(8,128)S(1)}, u32[]{:S(2)}, u32[]{:S(2)}) collective-permute-start(f32[1024,128]{1,0:T(8,128)S(1)} %collective-permute-done), channel_id=1, source_target_pairs={{0,4},{4,8},{8,12},{12,16},{16,20},{20,24},{24,28},{28,0},{1,5},{5... | collective-permute-start | bytes 1572872 | tf_op jit(solution)/shard_map/ppermute | solution.py:18
  151.6 19.6 %collective-permute-start.3 = (f32[1024,128]{1,0:T(8,128)S(1)}, f32[1024,128]{1,0:T(8,128)S(1)}, u32[]{:S(2)}, u32[]{:S(2)}) collective-permute-start(f32[1024,128]{1,0:T(8,128)S(1)} %collective-permute-done.1), channel_id=1, source_target_pairs={{0,28},{4,0},{8,4},{12,8},{16,12},{20,16},{24,20},{28,24},{1,29},{... | collective-permute-start | bytes 1572872 | tf_op jit(solution)/shard_map/ppermute | solution.py:23
  167.3 15.8 %collective-permute-start.4 = (f32[1024,128]{1,0:T(8,128)S(1)}, f32[1024,128]{1,0:T(8,128)S(1)}, u32[]{:S(2)}, u32[]{:S(2)}) collective-permute-start(f32[1024,128]{1,0:T(8,128)S(1)} %collective-permute-done.2), channel_id=1, source_target_pairs={{0,4},{4,8},{8,12},{12,16},{16,20},{20,24},{24,28},{28,0},{1,5},{5... | collective-permute-start | bytes 1572872 | tf_op jit(solution)/shard_map/ppermute | solution.py:18
  171.1 15.3 %collective-permute-start.5 = (f32[1024,128]{1,0:T(8,128)S(1)}, f32[1024,128]{1,0:T(8,128)S(1)}, u32[]{:S(2)}, u32[]{:S(2)}) collective-permute-start(f32[1024,128]{1,0:T(8,128)S(1)} %collective-permute-done.3), channel_id=1, source_target_pairs={{0,28},{4,0},{8,4},{12,8},{16,12},{20,16},{24,20},{28,24},{1,29},{... | collective-permute-start | bytes 1572872 | tf_op jit(solution)/shard_map/ppermute | solution.py:23
  183.1 10.4 %collective-permute-start.6 = (f32[1024,128]{1,0:T(8,128)S(1)}, f32[1024,128]{1,0:T(8,128)S(1)}, u32[]{:S(2)}, u32[]{:S(2)}) collective-permute-start(f32[1024,128]{1,0:T(8,128)S(1)} %collective-permute-done.4), channel_id=1, source_target_pairs={{0,4},{4,8},{8,12},{12,16},{16,20},{20,24},{24,28},{28,0},{1,5},{5... | collective-permute-start | bytes 1572872 | tf_op jit(solution)/shard_map/ppermute | solution.py:18
Sparse Core Ops, SparseCore 0:
  32.4 56.8 all-reduce.2
  92.8 44.3 all-reduce.4
